TPU v7x, 32 devices: a whole 2x2x4 slice. The times are simulated.
32 devices in a mesh: prow: 4 (over y, core), pcol: 8 (over z, x).
Axes of the slice: x: 2, y: 2, z: 4, core: 2. Of those that a mesh axis runs over, the one named last changes fastest.
Arguments:
- ainv: bfloat16 [8192, 8192], P('prow', 'pcol'), may hold values from -6 to 6
- panels: bfloat16 [3, 8192, 128], P(None, ('prow', 'pcol')), may hold values from -0.0625 to 0.0625
- structure: int32 [3, 64], replicated, may hold values from 0 to 1, as said below
- dinv: float32 [3, 128, 128], replicated, may hold values from -6 to 6
- couple: bfloat16 [2, 128, 128], replicated, may hold values from -0.5 to 0.5
Outputs:
- inv_panels: float32 [3, 8192, 128], P(None, ('prow', 'pcol'))
- inv_parent: float32 [2, 128, 128], replicated
- inv_diag: float32 [3, 128, 128], replicated
Inputs may be any that keep to these rules, and one draw needn't show every extreme that they name: Entries are 0 or 1; a block in the structure of step k+1 is also in that of step k.
All inputs are finite; a program needn't handle non-finite values.
Results may differ from a plain program's by a relative error of at most 0.0003.
Values may be sent and summed in bfloat16 or wider, within the bound.
No kernel may reach another device: no remote copies, remote signals or barrier semaphores. Data moves between devices by JAX's collectives and lax.ppermute only.
A program may use at most 64 MiB of HBM per device.

v0:
```python
import jax
import jax.numpy as jnp
from jax import lax
from jax.sharding import PartitionSpec as P


def broadcast(value, axis, source):
    kept = jnp.where(lax.axis_index(axis) == source, value, 0).astype(value.dtype)
    return lax.psum(kept, axis)


def shards(ainv, panels, structure, dinv, couple):
    high = lax.Precision.HIGHEST
    n_col = lax.axis_size("pcol")
    seg_rows = panels.shape[1]
    width_cols = panels.shape[2]
    sections = panels.shape[0]
    col_span = ainv.shape[1]
    height = ainv.shape[0]
    flat_index = lax.axis_index("prow") * n_col + lax.axis_index("pcol")
    row_ids = flat_index * seg_rows + jnp.arange(seg_rows, dtype=jnp.int32)
    block_ids = jnp.arange(structure.shape[1], dtype=jnp.int32)
    onehot = (row_ids[:, None] // width_cols == block_ids[None, :]).astype(jnp.float32)
    live_rows = jnp.einsum("rb,kb->kr", onehot, structure.astype(jnp.float32))
    factor = panels * live_rows[:, :, None].astype(jnp.bfloat16)
    column = lax.axis_index("pcol")
    offset = column * col_span % height
    owner = column * col_span // height
    products = []
    for section in range(sections):
        gathered = lax.all_gather(factor[section], "pcol", axis=0, tiled=True)
        wanted = lax.dynamic_slice_in_dim(gathered, offset, col_span, 0)
        received = broadcast(wanted, "prow", owner)

        def single_term(row_start, row_count, panel_cols=received):
            return jnp.dot(ainv, panel_cols, preferred_element_type=jnp.float32)

        products.append(
            lax.psum_scatter(
                single_term(jnp.int32(0), seg_rows * lax.axis_size("pcol")),
                "pcol",
                scatter_dimension=0,
                tiled=True,
            )
        )
    factor_wide = factor.astype(jnp.float32)
    couple_wide = couple.astype(jnp.float32)
    first_block = -products[0] * live_rows[0][:, None]
    first_local = jnp.dot(factor_wide[0].T, first_block, precision=high)
    diag_now = dinv[0] - lax.psum(first_local, ("prow", "pcol"))
    blocks_out = [first_block]
    diag_out = [diag_now]
    cross_out = []
    for section in range(1, sections):
        previous = blocks_out[-1]
        current = (
            -(products[section] + jnp.dot(previous, couple_wide[section - 1], precision=high))
            * live_rows[section][:, None]
        )
        own_term = jnp.dot(factor_wide[section].T, current, precision=high)
        cross_term = jnp.dot(previous.T, factor_wide[section], precision=high)
        own_sum, cross_sum = lax.psum((own_term, cross_term), ("prow", "pcol"))
        cross = -(cross_sum + jnp.dot(diag_now, couple_wide[section - 1], precision=high))
        diag_now = (
            dinv[section] - own_sum - jnp.dot(couple_wide[section - 1].T, cross, precision=high)
        )
        blocks_out.append(current)
        cross_out.append(cross)
        diag_out.append(diag_now)
    return (jnp.stack(blocks_out), jnp.stack(cross_out), jnp.stack(diag_out))


def solution(mesh):
    return jax.shard_map(
        shards,
        mesh=mesh,
        in_specs=(P("prow", "pcol"), P(None, ("prow", "pcol"), None), P(), P(), P()),
        out_specs=(P(None, ("prow", "pcol"), None), P(), P()),
        check_vma=False,
    )
```

profile of v0, /device:TPU:8, one launch (start us, length us, event | category | flops | bytes accessed | tf_op | source)
XLA Modules:
  0.0 495.4 jit_solution(17148334694424355662)
XLA Ops:
  7.3 0.9 fusion.45
  8.2 1.1 broadcast_multiply_fusion
  9.3 28.8 %all-gather = bf16[1,2048,128]{2,1,0:T(8,128)(2,1)S(1)} all-gather(bf16[1,256,128]{2,1,0:T(8,128)(2,1)S(1)} %get-tuple-element.14), channel_id=2, replica_groups=mesh['prow'=4,'pcol'=8] {'pcol'}, dimensions={1}, use_global_device_ids=true | all-gather | bytes 589824 | tf_op jit(solution)/shard_map/all_gather | solution.py:31
  38.0 31.6 %all-gather.2 = bf16[1,2048,128]{2,1,0:T(8,128)(2,1)S(1)} all-gather(bf16[1,256,128]{2,1,0:T(8,128)(2,1)S(1)} %get-tuple-element.15), channel_id=4, replica_groups=mesh['prow'=4,'pcol'=8] {'pcol'}, dimensions={1}, use_global_device_ids=true | all-gather | bytes 589824 | tf_op jit(solution)/shard_map/all_gather | solution.py:31
  69.6 0.8 select_bitcast_fusion.2
  70.4 0.8 select_bitcast_fusion
  71.2 31.1 %all-gather.1 = bf16[1,2048,128]{2,1,0:T(8,128)(2,1)S(1)} all-gather(bf16[1,256,128]{2,1,0:T(8,128)(2,1)S(1)} %get-tuple-element.16), channel_id=3, replica_groups=mesh['prow'=4,'pcol'=8] {'pcol'}, dimensions={1}, use_global_device_ids=true | all-gather | bytes 589824 | tf_op jit(solution)/shard_map/all_gather | solution.py:31
  102.3 0.8 select_bitcast_fusion.1
  103.1 39.1 %all-reduce.7.cloned.1.call-done = (bf16[1024,128]{1,0:T(8,128)(2,1)}, bf16[1024,128]{1,0:T(8,128)(2,1)}, bf16[1024,128]{1,0:T(8,128)(2,1)}) async-done(((bf16[1024,128]{1,0:T(8,128)(2,1)}, bf16[1024,128]{1,0:T(8,128)(2,1)}, bf16[1024,128]{1,0:T(8,128)(2,1)}), (bf16[1024,128]{1,0:T(8,128)(2,1)}, bf16[1024,128]{1,0:T(8,128)(2,1)}, bf16[1024,128]{1,0:T(8,128)(2,1)})) %all-reduce.7.cloned.1.call-update) | async-done | bytes 786448 | tf_op jit(solution)/shard_map/psum | solution.py:9
  142.2 4.8 convolution_bitcast_fusion.1
  147.1 4.7 convolution_bitcast_fusion.2
  151.9 4.8 convolution_bitcast_fusion
  156.7 54.9 %reduce-scatter.6.cloned.1.call-done = f32[256,128]{0,1:T(8,128)} async-done(((f32[2048,128]{0,1:T(8,128)}), f32[256,128]{0,1:T(8,128)}) %reduce-scatter.6.cloned.1.call-update) | async-done | bytes 131088 | tf_op jit(solution)/shard_map/reduce_scatter | solution.py:39
  211.7 67.1 %reduce-scatter.4.cloned.1.call-done = f32[256,128]{0,1:T(8,128)} async-done(((f32[2048,128]{0,1:T(8,128)}), f32[256,128]{0,1:T(8,128)}) %reduce-scatter.4.cloned.1.call-update) | async-done | bytes 131088 | tf_op jit(solution)/shard_map/reduce_scatter | solution.py:39
  278.8 1.2 fusion.2
  280.0 0.9 fusion.18
  280.9 0.8 fusion.12
  281.7 64.0 %reduce-scatter.8.cloned.1.call-done = f32[256,128]{0,1:T(8,128)} async-done(((f32[2048,128]{0,1:T(8,128)}), f32[256,128]{0,1:T(8,128)}) %reduce-scatter.8.cloned.1.call-update) | async-done | bytes 131088 | tf_op jit(solution)/shard_map/reduce_scatter | solution.py:39
  345.7 1.2 fusion.3
  346.9 0.9 fusion.14
  347.8 1.7 fusion.10
  349.5 1.8 fusion.9
  351.3 0.9 fusion.11
  352.3 0.9 copy.12
  353.2 129.2 %all-reduce.5.cloned.1.call-done = (f32[128,128]{1,0:T(8,128)}, f32[128,128]{1,0:T(8,128)}, f32[128,128]{1,0:T(8,128)}, f32[128,128]{1,0:T(8,128)}, f32[128,128]{1,0:T(8,128)}) async-done(((f32[128,128]{1,0:T(8,128)}, f32[128,128]{1,0:T(8,128)}, f32[128,128]{1,0:T(8,128)}, f32[128,128]{1,0:T(8,128)}, f32[128,128]{1,0:T(8,128)}), (f32[128,128]{1,0:T(8,128)}, f32[128,128]{1,0:T(8,128)}, f32[128,128]{1,0:T(8,128)}, ...) | async-done | bytes 327696 | tf_op jit(solution)/shard_map/psum | solution.py:62
  482.4 0.8 fusion.30
  483.2 1.0 fusion.8
  484.3 1.1 fusion.7
  485.4 1.0 fusion.6
  486.4 1.1 fusion.5
  487.5 0.7 pad_maximum_fusion.2
  488.2 0.7 pad_maximum_fusion.1
  (22 shorter events, 0.4 us)
Async XLA Ops:
  7.2 135.0 %all-reduce.7.cloned.1.call-start = ((), (), s32[]{:S(2)}) async-start(), calls=%async_computation.7 | async-start | bytes 1572864 | tf_op jit(solution)/shard_map/psum | solution.py:9
  103.1 108.6 %reduce-scatter.6.cloned.1.call-start = ((), (), s32[]{:S(2)}) async-start(), calls=%async_computation.4 | async-start | bytes 1179648 | tf_op jit(solution)/shard_map/reduce_scatter | solution.py:39
  142.2 4.9 copy-start.3
  147.0 4.9 copy-start.2
  147.0 131.7 %reduce-scatter.4.cloned.1.call-start = ((), (), s32[]{:S(2)}) async-start(), calls=%async_computation.3 | async-start | bytes 1179648 | tf_op jit(solution)/shard_map/reduce_scatter | solution.py:39
  151.8 127.0 %copy-start = (bf16[2,128,128]{2,1,0:T(8,128)(2,1)S(1)}, bf16[2,128,128]{2,1,0:T(8,128)(2,1)}, u32[]{:S(2)}) copy-start(bf16[2,128,128]{2,1,0:T(8,128)(2,1)} %param.9) | copy-start | bytes 196612
  151.8 193.9 %reduce-scatter.8.cloned.1.call-start = ((), (), s32[]{:S(2)}) async-start(), calls=%async_computation.5 | async-start | bytes 1179648 | tf_op jit(solution)/shard_map/reduce_scatter | solution.py:39
  151.9 330.5 %copy-start.1 = (f32[3,128,128]{2,1,0:T(8,128)S(1)}, f32[3,128,128]{2,1,0:T(8,128)}, u32[]{:S(2)}) copy-start(f32[3,128,128]{2,1,0:T(8,128)} %param.8) | copy-start | bytes 589828
  156.7 325.7 %all-reduce.5.cloned.1.call-start = ((), (), s32[]{:S(2)}) async-start(), calls=%async_computation.6 | async-start | bytes 655360 | tf_op jit(solution)/shard_map/psum | solution.py:62
Sparse Core Ops, SparseCore 0:
  103.2 38.9 all-reduce.6
  147.2 64.4 reduce-scatter.5
  215.1 63.6 reduce-scatter.3
  282.0 63.6 reduce-scatter.7
  352.4 129.9 all-reduce.4
where the time goes:
time: 496 us; the launch traced here: 495 us
  waiting for transfers between devices  354 us (71%)
  blocking collectives  91.5 us (18%)
  matrix products  27.9 us (6%)
  between operations  13.9 us (3%)
  other arithmetic  6.52 us (1%)
    reduce_scatter x3, waiting for transfers between devices, shards(): lax.psum_scatter(single_term(jnp.int32(0), seg_rows * lax.axis_size('pcol...  186 us
    psum x1, waiting for transfers between devices, shards(): own_sum, cross_sum = lax.psum((own_term, cross_term), ('prow', 'pcol'))  129 us
    all_gather x3, blocking collectives, shards(): gathered = lax.all_gather(factor[section], 'pcol', axis=0, tiled=True)  91.5 us
    psum x1, waiting for transfers between devices, broadcast(): return lax.psum(kept, axis)  39.1 us
    dot_general x3, matrix products, single_term(): return jnp.dot(ainv, panel_cols, preferred_element_type=jnp.float32)  14.3 us
  transfers between devices with their start and end apart: 5, of which 5 were waited for; matrix products, arithmetic and copies ran while one was open for 3% of the time, Pallas kernels for 0%

commit v1 on v0

--- a/solution.py
+++ b/solution.py
@@ -28,7 +28,14 @@
     owner = column * col_span // height
     products = []
     for section in range(sections):
-        gathered = lax.all_gather(factor[section], "pcol", axis=0, tiled=True)
+        ways, here = (lax.axis_size("pcol"), lax.axis_index("pcol"))
+        gathered, reach = (factor[section], 1)
+        while reach < ways:
+            theirs = lax.ppermute(gathered, "pcol", [(d, d ^ reach) for d in range(ways)])
+            mine_first = jnp.concatenate([gathered, theirs], axis=0)
+            theirs_first = jnp.concatenate([theirs, gathered], axis=0)
+            gathered = jnp.where(here & reach == 0, mine_first, theirs_first)
+            reach = 2 * reach
         wanted = lax.dynamic_slice_in_dim(gathered, offset, col_span, 0)
         received = broadcast(wanted, "prow", owner)
 

time: 496 us -> 445 us (0.90)
  blocking collectives: 91.5 us -> 0 us
  waiting for transfers between devices: 354 us -> 377 us
  starting transfers between devices: 0.21 us -> 15.6 us
    all_gather x3 -> x0, blocking collectives: 91.5 us -> none  [shards(): gathered = lax.all_gather(factor[section], 'pcol', axis=0, tiled=True)]
    ppermute x0 -> x9, waiting for transfers between devices: none -> 24.9 us  [shards(): lax.ppermute(gathered, 'pcol', [(d, d ^ reach) for d in range(ways)])]
    ppermute x0 -> x9, starting transfers between devices: none -> 15.4 us  [shards(): lax.ppermute(gathered, 'pcol', [(d, d ^ reach) for d in range(ways)])]
  transfers between devices with their start and end apart: 5 -> 14, of which waited for: 5 -> 11; matrix products, arithmetic and copies ran while one was open for 3% -> 4% of each run, Pallas kernels for 0% -> 0%
where the time goes in v1:
time: 445 us
  waiting for transfers between devices  377 us (85%)
  matrix products  27.9 us (6%)
  starting transfers between devices  15.6 us (4%)
  between operations  13.9 us (3%)
  other arithmetic  9.42 us (2%)
    reduce_scatter x3, waiting for transfers between devices, shards(): lax.psum_scatter(single_term(jnp.int32(0), seg_rows * lax.axis_size('pcol...  186 us
    psum x1, waiting for transfers between devices, shards(): own_sum, cross_sum = lax.psum((own_term, cross_term), ('prow', 'pcol'))  129 us
    psum x1, waiting for transfers between devices, broadcast(): return lax.psum(kept, axis)  36.7 us
    ppermute x9, waiting for transfers between devices, shards(): lax.ppermute(gathered, 'pcol', [(d, d ^ reach) for d in range(ways)])  24.9 us
    ppermute x9, starting transfers between devices, shards(): lax.ppermute(gathered, 'pcol', [(d, d ^ reach) for d in range(ways)])  15.4 us
    dot_general x3, matrix products, single_term(): return jnp.dot(ainv, panel_cols, preferred_element_type=jnp.float32)  14.3 us
  transfers between devices with their start and end apart: 14, of which 11 were waited for; matrix products, arithmetic and copies ran while one was open for 4% of the time, Pallas kernels for 0%

profile of v1, /device:TPU:8, one launch (start us, length us, event | category | flops | bytes accessed | tf_op | source)
XLA Modules:
  0.0 444.7 jit_solution(8191397903630953974)
XLA Ops:
  8.1 1.1 broadcast_multiply_fusion
  9.3 1.6 collective-permute-start
  11.4 1.5 collective-permute-start.3
  12.8 1.4 collective-permute-done
  14.3 1.4 collective-permute-done.6
  16.5 1.4 collective-permute-start.4
  17.9 2.8 collective-permute-done.1
  20.8 4.5 %collective-permute-start.2 = (bf16[1024,128]{1,0:T(8,128)(2,1)S(1)}, bf16[1024,128]{1,0:T(8,128)(2,1)S(1)}, u32[]{:S(2)}, u32[]{:S(2)}) collective-permute-start(bf16[1024,128]{1,0:T(8,128)(2,1)S(1)} %maximum_select_fusion), channel_id=1, source_target_pairs={{0,4},{1,5},{2,6},{3,7},{4,0},{5,1},{6,2},{7,3},{8,12},{9,13},{10,... | collective-permute-start | bytes 786440 | tf_op jit(solution)/shard_map/ppermute | solution.py:34
  25.4 3.7 collective-permute-start.8
  29.2 1.3 collective-permute-start.5
  30.5 15.1 %collective-permute-done.2 = bf16[1024,128]{1,0:T(8,128)(2,1)S(1)} collective-permute-done((bf16[1024,128]{1,0:T(8,128)(2,1)S(1)}, bf16[1024,128]{1,0:T(8,128)(2,1)S(1)}, u32[]{:S(2)}, u32[]{:S(2)}) %collective-permute-start.2) | collective-permute-done | bytes 262176 | tf_op jit(solution)/shard_map/ppermute | solution.py:34
  45.6 1.6 fusion.19
  47.2 3.1 collective-permute-done.8
  50.3 1.6 fusion.11
  51.9 1.2 collective-permute-done.5
  53.1 1.6 fusion.15
  54.8 36.7 %all-reduce.7.cloned.1.call-done = (bf16[1024,128]{1,0:T(8,128)(2,1)}, bf16[1024,128]{1,0:T(8,128)(2,1)}, bf16[1024,128]{1,0:T(8,128)(2,1)}) async-done(((bf16[1024,128]{1,0:T(8,128)(2,1)}, bf16[1024,128]{1,0:T(8,128)(2,1)}, bf16[1024,128]{1,0:T(8,128)(2,1)}), (bf16[1024,128]{1,0:T(8,128)(2,1)}, bf16[1024,128]{1,0:T(8,128)(2,1)}, bf16[1024,128]{1,0:T(8,128)(2,1)})) %all-reduce.7.cloned.1.call-update) | async-done | bytes 786448 | tf_op jit(solution)/shard_map/psum | solution.py:9
  91.5 4.8 %convolution_bitcast_fusion.1 = f32[2048,128]{0,1:T(8,128)} fusion(bf16[1024,128]{1,0:T(8,128)(2,1)} %get-tuple-element.12, bf16[2048,1024]{1,0:T(8,128)(2,1)} %param.5), kind=kOutput, calls=%fused_computation.1 | convolution fusion | flops 536870912 | bytes 5505024 | tf_op jit(solution)/shard_map/dot_general | solution.py:43
  96.4 4.7 %convolution_bitcast_fusion.2 = f32[2048,128]{0,1:T(8,128)} fusion(bf16[1024,128]{1,0:T(8,128)(2,1)S(1)} %copy-done.3, bf16[2048,1024]{1,0:T(8,128)(2,1)} %param.5), kind=kOutput, calls=%fused_computation.2 | convolution fusion | flops 536870912 | bytes 5505024 | tf_op jit(solution)/shard_map/dot_general | solution.py:43
  101.2 4.7 %convolution_bitcast_fusion = f32[2048,128]{0,1:T(8,128)} fusion(bf16[1024,128]{1,0:T(8,128)(2,1)S(1)} %copy-done.2, bf16[2048,1024]{1,0:T(8,128)(2,1)} %param.5), kind=kOutput, calls=%fused_computation | convolution fusion | flops 536870912 | bytes 5505024 | tf_op jit(solution)/shard_map/dot_general | solution.py:43
  106.0 55.0 %reduce-scatter.6.cloned.1.call-done = f32[256,128]{0,1:T(8,128)} async-done(((f32[2048,128]{0,1:T(8,128)}), f32[256,128]{0,1:T(8,128)}) %reduce-scatter.6.cloned.1.call-update) | async-done | bytes 131088 | tf_op jit(solution)/shard_map/reduce_scatter | solution.py:46
  160.9 67.2 %reduce-scatter.4.cloned.1.call-done = f32[256,128]{0,1:T(8,128)} async-done(((f32[2048,128]{0,1:T(8,128)}), f32[256,128]{0,1:T(8,128)}) %reduce-scatter.4.cloned.1.call-update) | async-done | bytes 131088 | tf_op jit(solution)/shard_map/reduce_scatter | solution.py:46
  228.1 1.2 fusion.2
  231.1 64.0 %reduce-scatter.8.cloned.1.call-done = f32[256,128]{0,1:T(8,128)} async-done(((f32[2048,128]{0,1:T(8,128)}), f32[256,128]{0,1:T(8,128)}) %reduce-scatter.8.cloned.1.call-update) | async-done | bytes 131088 | tf_op jit(solution)/shard_map/reduce_scatter | solution.py:46
  295.1 1.2 fusion.3
  297.1 1.7 fusion.22
  298.9 1.8 fusion.21
  302.5 129.2 %all-reduce.5.cloned.1.call-done = (f32[128,128]{1,0:T(8,128)}, f32[128,128]{1,0:T(8,128)}, f32[128,128]{1,0:T(8,128)}, f32[128,128]{1,0:T(8,128)}, f32[128,128]{1,0:T(8,128)}) async-done(((f32[128,128]{1,0:T(8,128)}, f32[128,128]{1,0:T(8,128)}, f32[128,128]{1,0:T(8,128)}, f32[128,128]{1,0:T(8,128)}, f32[128,128]{1,0:T(8,128)}), (f32[128,128]{1,0:T(8,128)}, f32[128,128]{1,0:T(8,128)}, f32[128,128]{1,0:T(8,128)}, ...) | async-done | bytes 327696 | tf_op jit(solution)/shard_map/psum | solution.py:69
  432.6 1.0 fusion.8
  433.6 1.1 fusion.7
  434.7 1.0 fusion.6
  435.7 1.1 fusion.5
  (43 shorter events, 9.6 us)
Async XLA Ops:
  7.2 84.3 %all-reduce.7.cloned.1.call-start = ((), (), s32[]{:S(2)}) async-start(), calls=%async_computation.7 | async-start | bytes 1572864 | tf_op jit(solution)/shard_map/psum | solution.py:9
  9.3 5.0 %collective-permute-start = (bf16[256,128]{1,0:T(8,128)(2,1)S(1)}, bf16[256,128]{1,0:T(8,128)(2,1)S(1)}, u32[]{:S(2)}, u32[]{:S(2)}) collective-permute-start(bf16[256,128]{1,0:T(8,128)(2,1)S(1)} %get-tuple-element.14), channel_id=1, source_target_pairs={{0,1},{1,0},{2,3},{3,2},{4,5},{5,4},{6,7},{7,6},{8,9},{9,8},{10,11... | collective-permute-start | bytes 196616 | tf_op jit(solution)/shard_map/ppermute | solution.py:34
  10.8 4.9 %collective-permute-start.6 = (bf16[256,128]{1,0:T(8,128)(2,1)S(1)}, bf16[256,128]{1,0:T(8,128)(2,1)S(1)}, u32[]{:S(2)}, u32[]{:S(2)}) collective-permute-start(bf16[256,128]{1,0:T(8,128)(2,1)S(1)} %get-tuple-element.15), channel_id=1, source_target_pairs={{0,1},{1,0},{2,3},{3,2},{4,5},{5,4},{6,7},{7,6},{8,9},{9,8},{10,11... | collective-permute-start | bytes 196616 | tf_op jit(solution)/shard_map/ppermute | solution.py:34
  11.4 5.1 %collective-permute-start.3 = (bf16[256,128]{1,0:T(8,128)(2,1)S(1)}, bf16[256,128]{1,0:T(8,128)(2,1)S(1)}, u32[]{:S(2)}, u32[]{:S(2)}) collective-permute-start(bf16[256,128]{1,0:T(8,128)(2,1)S(1)} %get-tuple-element.16), channel_id=1, source_target_pairs={{0,1},{1,0},{2,3},{3,2},{4,5},{5,4},{6,7},{7,6},{8,9},{9,8},{10,11... | collective-permute-start | bytes 196616 | tf_op jit(solution)/shard_map/ppermute | solution.py:34
  14.3 6.4 %collective-permute-start.1 = (bf16[512,128]{1,0:T(8,128)(2,1)S(1)}, bf16[512,128]{1,0:T(8,128)(2,1)S(1)}, u32[]{:S(2)}, u32[]{:S(2)}) collective-permute-start(bf16[512,128]{1,0:T(8,128)(2,1)S(1)} %maximum_select_fusion.3), channel_id=1, source_target_pairs={{0,2},{1,3},{2,0},{3,1},{4,6},{5,7},{6,4},{7,5},{8,10},{9,11},{10,... | collective-permute-start | bytes 393224 | tf_op jit(solution)/shard_map/ppermute | solution.py:34
  15.7 9.6 %collective-permute-start.7 = (bf16[512,128]{1,0:T(8,128)(2,1)S(1)}, bf16[512,128]{1,0:T(8,128)(2,1)S(1)}, u32[]{:S(2)}, u32[]{:S(2)}) collective-permute-start(bf16[512,128]{1,0:T(8,128)(2,1)S(1)} %maximum_select_fusion.5), channel_id=1, source_target_pairs={{0,2},{1,3},{2,0},{3,1},{4,6},{5,7},{6,4},{7,5},{8,10},{9,11},{10,... | collective-permute-start | bytes 393224 | tf_op jit(solution)/shard_map/ppermute | solution.py:34
  16.5 12.6 %collective-permute-start.4 = (bf16[512,128]{1,0:T(8,128)(2,1)S(1)}, bf16[512,128]{1,0:T(8,128)(2,1)S(1)}, u32[]{:S(2)}, u32[]{:S(2)}) collective-permute-start(bf16[512,128]{1,0:T(8,128)(2,1)S(1)} %maximum_select_fusion.4), channel_id=1, source_target_pairs={{0,2},{1,3},{2,0},{3,1},{4,6},{5,7},{6,4},{7,5},{8,10},{9,11},{10,... | collective-permute-start | bytes 393224 | tf_op jit(solution)/shard_map/ppermute | solution.py:34
  20.8 24.8 %collective-permute-start.2 = (bf16[1024,128]{1,0:T(8,128)(2,1)S(1)}, bf16[1024,128]{1,0:T(8,128)(2,1)S(1)}, u32[]{:S(2)}, u32[]{:S(2)}) collective-permute-start(bf16[1024,128]{1,0:T(8,128)(2,1)S(1)} %maximum_select_fusion), channel_id=1, source_target_pairs={{0,4},{1,5},{2,6},{3,7},{4,0},{5,1},{6,2},{7,3},{8,12},{9,13},{10,... | collective-permute-start | bytes 786440 | tf_op jit(solution)/shard_map/ppermute | solution.py:34
  25.4 24.9 %collective-permute-start.8 = (bf16[1024,128]{1,0:T(8,128)(2,1)S(1)}, bf16[1024,128]{1,0:T(8,128)(2,1)S(1)}, u32[]{:S(2)}, u32[]{:S(2)}) collective-permute-start(bf16[1024,128]{1,0:T(8,128)(2,1)S(1)} %maximum_select_fusion.2), channel_id=1, source_target_pairs={{0,4},{1,5},{2,6},{3,7},{4,0},{5,1},{6,2},{7,3},{8,12},{9,13},{10,... | collective-permute-start | bytes 786440 | tf_op jit(solution)/shard_map/ppermute | solution.py:34
  29.2 23.9 %collective-permute-start.5 = (bf16[1024,128]{1,0:T(8,128)(2,1)S(1)}, bf16[1024,128]{1,0:T(8,128)(2,1)S(1)}, u32[]{:S(2)}, u32[]{:S(2)}) collective-permute-start(bf16[1024,128]{1,0:T(8,128)(2,1)S(1)} %maximum_select_fusion.1), channel_id=1, source_target_pairs={{0,4},{1,5},{2,6},{3,7},{4,0},{5,1},{6,2},{7,3},{8,12},{9,13},{10,... | collective-permute-start | bytes 786440 | tf_op jit(solution)/shard_map/ppermute | solution.py:34
  54.7 106.2 %reduce-scatter.6.cloned.1.call-start = ((), (), s32[]{:S(2)}) async-start(), calls=%async_computation.4 | async-start | bytes 1179648 | tf_op jit(solution)/shard_map/reduce_scatter | solution.py:46
  91.5 4.9 %copy-start.3 = (bf16[1024,128]{1,0:T(8,128)(2,1)S(1)}, bf16[1024,128]{1,0:T(8,128)(2,1)}, u32[]{:S(2)}) copy-start(bf16[1024,128]{1,0:T(8,128)(2,1)} %get-tuple-element.13) | copy-start | bytes 786436
  96.3 4.9 %copy-start.2 = (bf16[1024,128]{1,0:T(8,128)(2,1)S(1)}, bf16[1024,128]{1,0:T(8,128)(2,1)}, u32[]{:S(2)}) copy-start(bf16[1024,128]{1,0:T(8,128)(2,1)} %get-tuple-element.11) | copy-start | bytes 786436
  96.3 131.8 %reduce-scatter.4.cloned.1.call-start = ((), (), s32[]{:S(2)}) async-start(), calls=%async_computation.3 | async-start | bytes 1179648 | tf_op jit(solution)/shard_map/reduce_scatter | solution.py:46
  101.1 127.1 %copy-start = (bf16[2,128,128]{2,1,0:T(8,128)(2,1)S(1)}, bf16[2,128,128]{2,1,0:T(8,128)(2,1)}, u32[]{:S(2)}) copy-start(bf16[2,128,128]{2,1,0:T(8,128)(2,1)} %param.9) | copy-start | bytes 196612
  101.1 194.0 %reduce-scatter.8.cloned.1.call-start = ((), (), s32[]{:S(2)}) async-start(), calls=%async_computation.5 | async-start | bytes 1179648 | tf_op jit(solution)/shard_map/reduce_scatter | solution.py:46
  101.2 330.6 %copy-start.1 = (f32[3,128,128]{2,1,0:T(8,128)S(1)}, f32[3,128,128]{2,1,0:T(8,128)}, u32[]{:S(2)}) copy-start(f32[3,128,128]{2,1,0:T(8,128)} %param.8) | copy-start | bytes 589828
  105.9 325.8 %all-reduce.5.cloned.1.call-start = ((), (), s32[]{:S(2)}) async-start(), calls=%async_computation.6 | async-start | bytes 655360 | tf_op jit(solution)/shard_map/psum | solution.py:69
Sparse Core Ops, SparseCore 0:
  54.9 36.5 all-reduce.6
  96.4 64.4 reduce-scatter.5
  164.4 63.7 reduce-scatter.3
  231.4 63.6 reduce-scatter.7
  301.7 129.9 all-reduce.4
